TPU v7x, 128 devices: a whole 4x4x4 slice. The times are simulated.
128 devices in a mesh: row: 8 (over z, core), col: 16 (over y, x).
Axes of the slice: x: 4, y: 4, z: 4, core: 2. Of those that a mesh axis runs over, the one named last changes fastest.
Arguments:
- hidden: bfloat16 [1408, 16384], P('col', 'row'), may hold values from -18 to 18
- gain_in: bfloat16 [1408], replicated, may hold values from 0.5 to 1.5
- w_query: bfloat16 [1408, 1408], P('col'), may hold values from -0.3125 to 0.3125
- w_pair: bfloat16 [2, 1408, 1408], P(None, 'col'), may hold values from -0.15625 to 0.15625
- kv_cache: bfloat16 [2, 1408, 16384], P(None, 'col', 'row'), may hold values from -103 to 103
- recompute_rows: int32 [8, 200], P('row'), may hold values from 0 to 2047, as said below
- segment_ids: int32 [16384], P('row'), may hold values from -1 to 1, as said below
- w_out: bfloat16 [1408, 1408], P('col'), may hold values from -0.3125 to 0.3125
- gain_merge: bfloat16 [1408], replicated, may hold values from 0.5 to 1.5
- w_merge: bfloat16 [4, 1408, 1408], P(None, 'col'), may hold values from -0.078125 to 0.078125
- requests: int32 [8, 16, 85], P('row'), may hold values from -1 to 511, as said below
Outputs:
- delivered: bfloat16 [8, 16, 85, 1408], P('row', 'col')
Inputs may be any that keep to these rules, and one draw needn't show every extreme that they name: `segment_ids`: ids do not fall along the tokens except to -1 for the padding at the end; every image covers a multiple of 4 tokens and starts at a multiple of 4. `recompute_rows`: the 200 offsets of one index of row are distinct. `requests`: for each index of row, the lists of all owners together name each of its 512 merged tokens exactly once; unused slots hold -1 and follow the used ones.
All inputs are finite; a program needn't handle non-finite values.
Results may differ from a plain program's by a relative error of at most 0.025.
The roundings to bfloat16 on the way count: a program that leaves them out, or rounds other values in their place, can miss the bound.
Values may be sent and summed in bfloat16 or wider, within the bound.
A program may use at most 128 MiB of HBM per device.

v0:
```python
import jax
import jax.numpy as jnp
from jax import lax
from jax.sharding import PartitionSpec as P

HD = 88
EPSILON = 1e-06
MASKED = -1e30
KEY_BLOCK = 1024


def on_device(
    hidden,
    gain_in,
    w_query,
    w_pair,
    kv_cache,
    recompute_rows,
    segment_ids,
    w_out,
    gain_merge,
    w_merge,
    requests,
):
    local_width, tok_rows = hidden.shape
    model_width = w_query.shape[1]
    n_col = model_width // local_width
    heads_here = local_width // HD
    score_scale = HD ** (-0.5)
    col_index = lax.axis_index("col")
    full_rows = lax.all_gather(hidden, "col", axis=0, tiled=True)
    out_weight = lax.all_gather(w_out, "col", axis=0, tiled=True)
    full_float = full_rows.astype(jnp.float32)
    in_mean = jnp.sum(full_float, axis=0, keepdims=True) / model_width
    in_square = jnp.sum(full_float * full_float, axis=0, keepdims=True) / model_width
    normed = (
        (full_float - in_mean)
        * lax.rsqrt(in_square - in_mean * in_mean + EPSILON)
        * gain_in.astype(jnp.float32)[:, None]
    ).astype(jnp.bfloat16)
    queries = jnp.dot(w_query, normed, preferred_element_type=jnp.float32).astype(jnp.bfloat16)
    picked_rows = recompute_rows[0]
    normed_picked = jnp.take(normed, picked_rows, axis=1)
    fresh_pairs = jnp.dot(
        w_pair.reshape(2 * local_width, model_width),
        normed_picked,
        preferred_element_type=jnp.float32,
    )
    fresh_pairs = fresh_pairs.astype(jnp.bfloat16).reshape(2, local_width, -1)
    keys_values = kv_cache.at[:, :, picked_rows].set(fresh_pairs)
    query_heads = queries.reshape(heads_here, HD, tok_rows)
    pair_local = jnp.concatenate(
        [keys_values.reshape(2 * local_width, tok_rows), segment_ids.astype(jnp.bfloat16)[None, :]],
        axis=0,
    )
    pair_all = lax.all_gather(pair_local, "row", axis=1, tiled=True)
    pair_rows = pair_all[: 2 * local_width].reshape(2, local_width, -1)
    segment_line = pair_all[2 * local_width].astype(jnp.int32)

    def take_block(carried, pair_block, segment_block):
        running_max, running_sum, weighted = carried
        key_block = pair_block[0].reshape(heads_here, HD, -1)
        value_block = pair_block[1].reshape(heads_here, HD, -1)
        scores = (
            jnp.einsum("hdq,hdk->hqk", query_heads, key_block, preferred_element_type=jnp.float32)
            * score_scale
        )
        allowed = (segment_ids[:, None] == segment_block[None, :])[None, :, :]
        new_max = jnp.maximum(running_max, jnp.max(jnp.where(allowed, scores, MASKED), axis=2))
        weights_exp = jnp.where(allowed, jnp.exp(scores - new_max[:, :, None]), 0.0)
        factor = jnp.exp(running_max - new_max)
        running_sum = running_sum * factor + jnp.sum(weights_exp, axis=2)
        product = jnp.einsum(
            "hqk,hdk->hdq",
            weights_exp.astype(jnp.bfloat16),
            value_block,
            preferred_element_type=jnp.float32,
        )
        weighted = weighted * factor[:, None, :] + product
        return (new_max, running_sum, weighted)

    starting = (
        jnp.full((heads_here, tok_rows), MASKED, jnp.float32),
        jnp.zeros((heads_here, tok_rows), jnp.float32),
        jnp.zeros((heads_here, HD, tok_rows), jnp.float32),
    )
    piece_rows = pair_rows.shape[2]
    whole_blocks = piece_rows // KEY_BLOCK

    def loop_body(block_index, loop_state):
        pair_block = lax.dynamic_slice_in_dim(pair_rows, block_index * KEY_BLOCK, KEY_BLOCK, 2)
        segment_block = lax.dynamic_slice_in_dim(
            segment_line, block_index * KEY_BLOCK, KEY_BLOCK, 0
        )
        return take_block(loop_state, pair_block, segment_block)

    running_max, running_sum, weighted = lax.fori_loop(0, whole_blocks, loop_body, starting)
    attended = (
        (weighted / running_sum[:, None, :]).astype(jnp.bfloat16).reshape(local_width, tok_rows)
    )
    chunk = tok_rows // n_col
    attended_chunk = lax.all_to_all(attended, "col", 1, 0, tiled=True)
    x_chunk = lax.dynamic_slice_in_dim(full_float, col_index * chunk, chunk, 1)
    projected = lax.dot_general(
        out_weight, attended_chunk, (((0,), (0,)), ((), ())), preferred_element_type=jnp.float32
    )
    updated = x_chunk + projected
    row_mean = jnp.sum(updated, axis=0, keepdims=True) / model_width
    row_square = jnp.sum(updated * updated, axis=0, keepdims=True) / model_width
    merger_chunk = (
        (updated - row_mean)
        * lax.rsqrt(row_square - row_mean * row_mean + EPSILON)
        * gain_merge.astype(jnp.float32)[:, None]
    ).astype(jnp.bfloat16)
    merger_in = lax.all_to_all(merger_chunk, "col", 0, 1, tiled=True)
    merged_rows = tok_rows // 4
    grouped = merger_in.reshape(local_width, merged_rows, 4)
    merged = jnp.einsum("cgi,icd->gd", grouped, w_merge, preferred_element_type=jnp.float32)
    merged_sum = lax.psum(merged.astype(jnp.bfloat16), "col")
    wanted_rows = lax.dynamic_index_in_dim(requests[0], col_index, 0, keepdims=False)
    is_valid = wanted_rows >= 0
    safe_index = jnp.where(is_valid, wanted_rows, 0)
    picked = jnp.where(is_valid[:, None], merged_sum[safe_index], jnp.zeros((), jnp.bfloat16))
    return picked.reshape(1, 1, picked.shape[0], model_width)


def solution(mesh):
    placed = (
        P("col", "row"),
        P(),
        P("col", None),
        P(None, "col", None),
        P(None, "col", "row"),
        P("row", None),
        P("row"),
        P("col", None),
        P(),
        P(None, "col", None),
        P("row", None, None),
    )
    return jax.shard_map(
        on_device,
        mesh=mesh,
        in_specs=placed,
        out_specs=P("row", "col", None, None),
        check_vma=False,
    )
```

profile of v0, /device:TPU:0, one launch (start us, length us, event | category | flops | bytes accessed | tf_op | source)
XLA Modules:
  0.0 532.2 jit_solution(17478060739190972676)
XLA Ops:
  12.5 58.2 %all-gather.4.cloned.1.call-done = bf16[1408,2048]{1,0:T(8,128)(2,1)} async-done(((bf16[88,2048]{1,0:T(8,128)(2,1)}), bf16[1408,2048]{1,0:T(8,128)(2,1)}) %all-gather.4.cloned.1.call-update) | async-done | bytes 5767184 | tf_op jit(solution)/shard_map/all_gather | solution.py:31
  70.7 8.3 %copy.31 = bf16[1408,2048]{0,1:T(8,128)(2,1)} copy(bf16[1408,2048]{1,0:T(8,128)(2,1)} %all-gather.4.cloned.1.call-done) | data formatting | bytes 11534336 | tf_op jit(solution)/shard_map/all_gather | solution.py:31
  93.1 6.9 %scatter_fusion = bf16[2,88,2048]{1,0,2:T(2,128)(2,1)S(1)} fusion(bf16[2,88,2048]{1,0,2:T(2,128)(2,1)S(1)} %copy.33, s32[200]{0:T(256)S(1)} %bitcast.125, bf16[200,2,88]{2,1,0:T(2,128)(2,1)S(1)} %bitcast.118), kind=kCustom, calls=%fused_computation.2 | custom fusion | bytes 212000 | tf_op jit(solution)/shard_map/scatter | solution.py:50
  107.2 34.4 %all-gather.6.cloned.1.call-done = bf16[177,16384]{1,0:T(8,128)(2,1)} async-done(((bf16[177,2048]{1,0:T(8,128)(2,1)}), bf16[177,16384]{1,0:T(8,128)(2,1)}) %all-gather.6.cloned.1.call-update) | async-done | bytes 5799952 | tf_op jit(solution)/shard_map/all_gather | solution.py:56
  141.7 5.8 %slice.29 = bf16[176,16384]{1,0:T(8,128)(2,1)} slice(bf16[177,16384]{1,0:T(8,128)(2,1)} %all-gather.6.cloned.1.call-done), slice={[0:176], [0:16384]} | slice | bytes 11534336 | tf_op jit(solution)/shard_map/slice | solution.py:57
  148.4 251.7 %while.18 = (s32[]{:T(128)}, f32[1,2048]{1,0:T(1,128)S(1)}, f32[1,2048]{1,0:T(1,128)S(1)}, f32[1,88,2048]{2,1,0:T(8,128)S(1)}, s32[2048]{0:T(1024)S(1)}, /*index...) while((s32[]{:T(128)}, f32[1,2048]{1,0:T(1,128)S(1)}, ...), condition=%wide.region_6.7_spmd.clone, body=%wide.region_3.0_spmd.clone.sunk | while | flops 768108544 | bytes 27504848 | solution.py:97
  148.5 5.6 %fusion.45 = (f32[2048]{0:T(1024)S(1)}, f32[1024,2048]{1,0:T(8,128)}) fusion(s32[2048]{0:T(1024)S(1)} %get-tuple-element.290, s32[1024]{0:T(1024)S(1)} %dynamic_slice.32, bf16[1,88,2048]{2,1,0:T(8,128)(2,1)S(1)} %get-tuple-element.293, bf16[2,88,16384]{2,1,0:T(8,128)(2,1)} %get-tuple-element.292, s32[]{:T(128)S(6)} %select_n.132), kind=kOutput, calls=%fused_computation.5.clone.1 | convolution fusion | flops 377485312 | bytes 8949764 | tf_op jit(solution)/shard_map/while/body/eval_jaxpr/hdq,hdk->hqk/dot_general | solution.py:65
  180.0 5.6 %fusion.45 = (f32[2048]{0:T(1024)S(1)}, f32[1024,2048]{1,0:T(8,128)}) fusion(s32[2048]{0:T(1024)S(1)} %get-tuple-element.290, s32[1024]{0:T(1024)S(1)} %dynamic_slice.32, bf16[1,88,2048]{2,1,0:T(8,128)(2,1)S(1)} %get-tuple-element.293, bf16[2,88,16384]{2,1,0:T(8,128)(2,1)} %get-tuple-element.292, s32[]{:T(128)S(6)} %select_n.132), kind=kOutput, calls=%fused_computation.5.clone.1 | convolution fusion | flops 377485312 | bytes 8949764 | tf_op jit(solution)/shard_map/while/body/eval_jaxpr/hdq,hdk->hqk/dot_general | solution.py:65
  211.6 5.6 %fusion.45 = (f32[2048]{0:T(1024)S(1)}, f32[1024,2048]{1,0:T(8,128)}) fusion(s32[2048]{0:T(1024)S(1)} %get-tuple-element.290, s32[1024]{0:T(1024)S(1)} %dynamic_slice.32, bf16[1,88,2048]{2,1,0:T(8,128)(2,1)S(1)} %get-tuple-element.293, bf16[2,88,16384]{2,1,0:T(8,128)(2,1)} %get-tuple-element.292, s32[]{:T(128)S(6)} %select_n.132), kind=kOutput, calls=%fused_computation.5.clone.1 | convolution fusion | flops 377485312 | bytes 8949764 | tf_op jit(solution)/shard_map/while/body/eval_jaxpr/hdq,hdk->hqk/dot_general | solution.py:65
  227.3 5.6 %fusion.45 = (f32[2048]{0:T(1024)S(1)}, f32[1024,2048]{1,0:T(8,128)}) fusion(s32[2048]{0:T(1024)S(1)} %get-tuple-element.290, s32[1024]{0:T(1024)S(1)} %dynamic_slice.32, bf16[1,88,2048]{2,1,0:T(8,128)(2,1)S(1)} %get-tuple-element.293, bf16[2,88,16384]{2,1,0:T(8,128)(2,1)} %get-tuple-element.292, s32[]{:T(128)S(6)} %select_n.132), kind=kOutput, calls=%fused_computation.5.clone.1 | convolution fusion | flops 377485312 | bytes 8949764 | tf_op jit(solution)/shard_map/while/body/eval_jaxpr/hdq,hdk->hqk/dot_general | solution.py:65
  243.0 5.6 %fusion.45 = (f32[2048]{0:T(1024)S(1)}, f32[1024,2048]{1,0:T(8,128)}) fusion(s32[2048]{0:T(1024)S(1)} %get-tuple-element.290, s32[1024]{0:T(1024)S(1)} %dynamic_slice.32, bf16[1,88,2048]{2,1,0:T(8,128)(2,1)S(1)} %get-tuple-element.293, bf16[2,88,16384]{2,1,0:T(8,128)(2,1)} %get-tuple-element.292, s32[]{:T(128)S(6)} %select_n.132), kind=kOutput, calls=%fused_computation.5.clone.1 | convolution fusion | flops 377485312 | bytes 8949764 | tf_op jit(solution)/shard_map/while/body/eval_jaxpr/hdq,hdk->hqk/dot_general | solution.py:65
  258.7 5.6 %fusion.45 = (f32[2048]{0:T(1024)S(1)}, f32[1024,2048]{1,0:T(8,128)}) fusion(s32[2048]{0:T(1024)S(1)} %get-tuple-element.290, s32[1024]{0:T(1024)S(1)} %dynamic_slice.32, bf16[1,88,2048]{2,1,0:T(8,128)(2,1)S(1)} %get-tuple-element.293, bf16[2,88,16384]{2,1,0:T(8,128)(2,1)} %get-tuple-element.292, s32[]{:T(128)S(6)} %select_n.132), kind=kOutput, calls=%fused_computation.5.clone.1 | convolution fusion | flops 377485312 | bytes 8949764 | tf_op jit(solution)/shard_map/while/body/eval_jaxpr/hdq,hdk->hqk/dot_general | solution.py:65
  274.4 5.6 %fusion.45 = (f32[2048]{0:T(1024)S(1)}, f32[1024,2048]{1,0:T(8,128)}) fusion(s32[2048]{0:T(1024)S(1)} %get-tuple-element.290, s32[1024]{0:T(1024)S(1)} %dynamic_slice.32, bf16[1,88,2048]{2,1,0:T(8,128)(2,1)S(1)} %get-tuple-element.293, bf16[2,88,16384]{2,1,0:T(8,128)(2,1)} %get-tuple-element.292, s32[]{:T(128)S(6)} %select_n.132), kind=kOutput, calls=%fused_computation.5.clone.1 | convolution fusion | flops 377485312 | bytes 8949764 | tf_op jit(solution)/shard_map/while/body/eval_jaxpr/hdq,hdk->hqk/dot_general | solution.py:65
  290.2 5.6 %fusion.45 = (f32[2048]{0:T(1024)S(1)}, f32[1024,2048]{1,0:T(8,128)}) fusion(s32[2048]{0:T(1024)S(1)} %get-tuple-element.290, s32[1024]{0:T(1024)S(1)} %dynamic_slice.32, bf16[1,88,2048]{2,1,0:T(8,128)(2,1)S(1)} %get-tuple-element.293, bf16[2,88,16384]{2,1,0:T(8,128)(2,1)} %get-tuple-element.292, s32[]{:T(128)S(6)} %select_n.132), kind=kOutput, calls=%fused_computation.5.clone.1 | convolution fusion | flops 377485312 | bytes 8949764 | tf_op jit(solution)/shard_map/while/body/eval_jaxpr/hdq,hdk->hqk/dot_general | solution.py:65
  305.9 5.6 %fusion.45 = (f32[2048]{0:T(1024)S(1)}, f32[1024,2048]{1,0:T(8,128)}) fusion(s32[2048]{0:T(1024)S(1)} %get-tuple-element.290, s32[1024]{0:T(1024)S(1)} %dynamic_slice.32, bf16[1,88,2048]{2,1,0:T(8,128)(2,1)S(1)} %get-tuple-element.293, bf16[2,88,16384]{2,1,0:T(8,128)(2,1)} %get-tuple-element.292, s32[]{:T(128)S(6)} %select_n.132), kind=kOutput, calls=%fused_computation.5.clone.1 | convolution fusion | flops 377485312 | bytes 8949764 | tf_op jit(solution)/shard_map/while/body/eval_jaxpr/hdq,hdk->hqk/dot_general | solution.py:65
  321.6 5.6 %fusion.45 = (f32[2048]{0:T(1024)S(1)}, f32[1024,2048]{1,0:T(8,128)}) fusion(s32[2048]{0:T(1024)S(1)} %get-tuple-element.290, s32[1024]{0:T(1024)S(1)} %dynamic_slice.32, bf16[1,88,2048]{2,1,0:T(8,128)(2,1)S(1)} %get-tuple-element.293, bf16[2,88,16384]{2,1,0:T(8,128)(2,1)} %get-tuple-element.292, s32[]{:T(128)S(6)} %select_n.132), kind=kOutput, calls=%fused_computation.5.clone.1 | convolution fusion | flops 377485312 | bytes 8949764 | tf_op jit(solution)/shard_map/while/body/eval_jaxpr/hdq,hdk->hqk/dot_general | solution.py:65
  337.3 5.6 %fusion.45 = (f32[2048]{0:T(1024)S(1)}, f32[1024,2048]{1,0:T(8,128)}) fusion(s32[2048]{0:T(1024)S(1)} %get-tuple-element.290, s32[1024]{0:T(1024)S(1)} %dynamic_slice.32, bf16[1,88,2048]{2,1,0:T(8,128)(2,1)S(1)} %get-tuple-element.293, bf16[2,88,16384]{2,1,0:T(8,128)(2,1)} %get-tuple-element.292, s32[]{:T(128)S(6)} %select_n.132), kind=kOutput, calls=%fused_computation.5.clone.1 | convolution fusion | flops 377485312 | bytes 8949764 | tf_op jit(solution)/shard_map/while/body/eval_jaxpr/hdq,hdk->hqk/dot_general | solution.py:65
  353.0 5.6 %fusion.45 = (f32[2048]{0:T(1024)S(1)}, f32[1024,2048]{1,0:T(8,128)}) fusion(s32[2048]{0:T(1024)S(1)} %get-tuple-element.290, s32[1024]{0:T(1024)S(1)} %dynamic_slice.32, bf16[1,88,2048]{2,1,0:T(8,128)(2,1)S(1)} %get-tuple-element.293, bf16[2,88,16384]{2,1,0:T(8,128)(2,1)} %get-tuple-element.292, s32[]{:T(128)S(6)} %select_n.132), kind=kOutput, calls=%fused_computation.5.clone.1 | convolution fusion | flops 377485312 | bytes 8949764 | tf_op jit(solution)/shard_map/while/body/eval_jaxpr/hdq,hdk->hqk/dot_general | solution.py:65
  368.7 5.6 %fusion.45 = (f32[2048]{0:T(1024)S(1)}, f32[1024,2048]{1,0:T(8,128)}) fusion(s32[2048]{0:T(1024)S(1)} %get-tuple-element.290, s32[1024]{0:T(1024)S(1)} %dynamic_slice.32, bf16[1,88,2048]{2,1,0:T(8,128)(2,1)S(1)} %get-tuple-element.293, bf16[2,88,16384]{2,1,0:T(8,128)(2,1)} %get-tuple-element.292, s32[]{:T(128)S(6)} %select_n.132), kind=kOutput, calls=%fused_computation.5.clone.1 | convolution fusion | flops 377485312 | bytes 8949764 | tf_op jit(solution)/shard_map/while/body/eval_jaxpr/hdq,hdk->hqk/dot_general | solution.py:65
  384.4 5.6 %fusion.45 = (f32[2048]{0:T(1024)S(1)}, f32[1024,2048]{1,0:T(8,128)}) fusion(s32[2048]{0:T(1024)S(1)} %get-tuple-element.290, s32[1024]{0:T(1024)S(1)} %dynamic_slice.32, bf16[1,88,2048]{2,1,0:T(8,128)(2,1)S(1)} %get-tuple-element.293, bf16[2,88,16384]{2,1,0:T(8,128)(2,1)} %get-tuple-element.292, s32[]{:T(128)S(6)} %select_n.132), kind=kOutput, calls=%fused_computation.5.clone.1 | convolution fusion | flops 377485312 | bytes 8949764 | tf_op jit(solution)/shard_map/while/body/eval_jaxpr/hdq,hdk->hqk/dot_general | solution.py:65
  401.1 6.9 %all-to-all-start = ((bf16[88,16,128]{2,0,1:T(8,128)(2,1)}), bf16[88,16,128]{2,0,1:T(8,128)(2,1)S(1)}, u32[]{:S(2)}, u32[]{:S(2)}) async-start(bf16[88,16,128]{2,0,1:T(8,128)(2,1)} %copy.35), calls=%async_computation | async-start | bytes 720896 | tf_op jit(solution)/shard_map/all_to_all | solution.py:102
  408.1 7.6 %convert_element_type.50 = f32[1408,2048]{0,1:T(8,128)} convert(bf16[1408,2048]{0,1:T(8,128)(2,1)} %copy.31) | non-fusion elementwise | flops 2883584 | bytes 17301504 | tf_op jit(solution)/shard_map/convert_element_type | solution.py:33
  421.7 14.1 %all_to_all.35 = bf16[16,88,128]{2,1,0:T(8,128)(2,1)S(1)} all-to-all(bf16[16,88,128]{2,1,0:T(8,128)(2,1)S(1)} %bitcast.114), channel_id=1, replica_groups=mesh['row'=8,'col'=16] {'col'}, dimensions={0} | all-to-all | bytes 720896 | tf_op jit(solution)/shard_map/all_to_all | solution.py:115
  439.6 82.8 %all-reduce.2.cloned.1.call-done = bf16[512,1408]{1,0:T(8,128)(2,1)} async-done(((bf16[512,1408]{1,0:T(8,128)(2,1)}), bf16[512,1408]{1,0:T(8,128)(2,1)}) %all-reduce.2.cloned.1.call-update) | async-done | bytes 1441808 | tf_op jit(solution)/shard_map/psum | solution.py:119
  (155 shorter events, 214.4 us)
Async XLA Ops:
  6.5 429.6 %copy-start = (bf16[4,88,1408]{2,1,0:T(8,128)(2,1)S(1)}, bf16[4,88,1408]{2,1,0:T(8,128)(2,1)}, u32[]{:S(2)}) copy-start(bf16[4,88,1408]{2,1,0:T(8,128)(2,1)} %param.22) | copy-start | bytes 2973700
  6.5 64.2 %all-gather.4.cloned.1.call-start = ((), (), s32[]{:S(2)}) async-start(), calls=%async_computation.2 | async-start | bytes 6127616 | tf_op jit(solution)/shard_map/all_gather | solution.py:31
  7.3 134.4 %all-gather.6.cloned.1.call-start = ((), (), s32[]{:S(2)}) async-start(), calls=%async_computation.3 | async-start | bytes 6782976 | tf_op jit(solution)/shard_map/all_gather | solution.py:56
  79.1 4.5 copy-start.1
  83.6 9.0 %copy-start.5 = (bf16[2,88,1408]{2,1,0:T(8,128)(2,1)S(1)}, bf16[2,88,1408]{2,1,0:T(8,128)(2,1)}, u32[]{:S(2)}) copy-start(bf16[2,88,1408]{2,1,0:T(8,128)(2,1)} %param.16) | copy-start | bytes 1486852
  87.5 15.0 %copy-start.3 = (bf16[88,1408]{1,0:T(8,128)(2,1)S(1)}, bf16[88,1408]{1,0:T(8,128)(2,1)}, u32[]{:S(2)}) copy-start(bf16[88,1408]{1,0:T(8,128)(2,1)} %param.15) | copy-start | bytes 743428
  101.8 313.8 %all-gather.8.cloned.1.call-start = ((), (), s32[]{:S(2)}) async-start(), calls=%async_computation.4 | async-start | bytes 4212736 | tf_op jit(solution)/shard_map/all_gather | solution.py:32
  102.5 45.9 %copy-start.2 = (s32[2048]{0:T(1024)S(1)}, s32[2048]{0:T(1024)}, u32[]{:S(2)}) copy-start(s32[2048]{0:T(1024)} %param.19) | copy-start | bytes 24580
  148.4 259.6 %copy-start.4 = (bf16[1408]{0:T(1024)(128)(2,1)S(1)}, bf16[1408]{0:T(1024)(128)(2,1)}, u32[]{:S(2)}) copy-start(bf16[1408]{0:T(1024)(128)(2,1)} %param.21) | copy-start | bytes 8452
  401.1 17.0 %all-to-all-start = ((bf16[88,16,128]{2,0,1:T(8,128)(2,1)}), bf16[88,16,128]{2,0,1:T(8,128)(2,1)S(1)}, u32[]{:S(2)}, u32[]{:S(2)}) async-start(bf16[88,16,128]{2,0,1:T(8,128)(2,1)} %copy.35), calls=%async_computation | async-start | bytes 720896 | tf_op jit(solution)/shard_map/all_to_all | solution.py:102
  408.0 114.4 %all-reduce.2.cloned.1.call-start = ((), (), s32[]{:S(2)}) async-start(), calls=%async_computation.5 | async-start | bytes 2883584 | tf_op jit(solution)/shard_map/psum | solution.py:119
Sparse Core Ops, SparseCore 0:
  9.5 61.1 all-gather.3
  101.9 39.7 all-gather.5
  143.8 50.4 all-gather.7
  438.4 83.9 all-reduce.1
where the time goes:
time: 534 us; the launch traced here: 532 us
  matrix products  187 us (35%)
  waiting for transfers between devices  179 us (34%)
  other arithmetic  97.5 us (18%)
  local copies, waits for them, and re-layouts  33.4 us (6%)
  blocking collectives  14.1 us (3%)
  between operations  13.4 us (3%)
  starting transfers between devices  7.17 us (1%)
    dot_general x16, matrix products, take_block(): jnp.einsum('hdq,hdk->hqk', query_heads, key_block, preferred_element_type...  89.9 us
    dot_general x16, matrix products, take_block(): jnp.einsum('hqk,hdk->hdq', weights_exp.astype(jnp.bfloat16), value_block,...  86.4 us
    psum x1, waiting for transfers between devices, on_device(): merged_sum = lax.psum(merged.astype(jnp.bfloat16), 'col')  82.8 us
    reduce_sum x16, other arithmetic, take_block(): running_sum = running_sum * factor + jnp.sum(weights_exp, axis=2)  73.4 us
    all_gather x1, waiting for transfers between devices, on_device(): full_rows = lax.all_gather(hidden, 'col', axis=0, tiled=True)  58.2 us
    all_gather x1, waiting for transfers between devices, on_device(): pair_all = lax.all_gather(pair_local, 'row', axis=1, tiled=True)  34.4 us
    all_to_all x1, blocking collectives, on_device(): merger_in = lax.all_to_all(merger_chunk, 'col', 0, 1, tiled=True)  14.1 us
  transfers between devices with their start and end apart: 5, of which 4 were waited for; matrix products, arithmetic and copies ran while one was open for 52% of the time, Pallas kernels for 0%

commit v1 on v0

--- a/solution.py
+++ b/solution.py
@@ -116,7 +116,9 @@
     merged_rows = tok_rows // 4
     grouped = merger_in.reshape(local_width, merged_rows, 4)
     merged = jnp.einsum("cgi,icd->gd", grouped, w_merge, preferred_element_type=jnp.float32)
-    merged_sum = lax.psum(merged.astype(jnp.bfloat16), "col")
+    block = merged.astype(jnp.bfloat16)
+    parts = lax.all_gather(block, "col")
+    merged_sum = jnp.sum(parts, axis=0)
     wanted_rows = lax.dynamic_index_in_dim(requests[0], col_index, 0, keepdims=False)
     is_valid = wanted_rows >= 0
     safe_index = jnp.where(is_valid, wanted_rows, 0)

time: 534 us -> 601 us (1.13)
  waiting for transfers between devices: 179 us -> 235 us
  other arithmetic: 97.5 us -> 110 us
    all_gather x0 -> x1, waiting for transfers between devices: none -> 139 us  [on_device(): parts = lax.all_gather(block, 'col')]
    psum x1 -> x0, waiting for transfers between devices: 82.8 us -> none  [on_device(): merged_sum = lax.psum(merged.astype(jnp.bfloat16), 'col')]
    reduce_sum x0 -> x1, other arithmetic: none -> 12.2 us  [on_device(): merged_sum = jnp.sum(parts, axis=0)]
  transfers between devices with their start and end apart: 5 -> 5, of which waited for: 4 -> 4; matrix products, arithmetic and copies ran while one was open for 52% -> 46% of each run, Pallas kernels for 0% -> 0%
where the time goes in v1:
time: 601 us; the launch traced here: 599 us
  waiting for transfers between devices  235 us (39%)
  matrix products  187 us (31%)
  other arithmetic  110 us (18%)
  local copies, waits for them, and re-layouts  31.7 us (5%)
  blocking collectives  14.1 us (2%)
  between operations  13.4 us (2%)
  starting transfers between devices  7.17 us (1%)
    all_gather x1, waiting for transfers between devices, on_device(): parts = lax.all_gather(block, 'col')  139 us
    dot_general x16, matrix products, take_block(): jnp.einsum('hdq,hdk->hqk', query_heads, key_block, preferred_element_type...  89.9 us
    dot_general x16, matrix products, take_block(): jnp.einsum('hqk,hdk->hdq', weights_exp.astype(jnp.bfloat16), value_block,...  86.4 us
    reduce_sum x16, other arithmetic, take_block(): running_sum = running_sum * factor + jnp.sum(weights_exp, axis=2)  73.4 us
    all_gather x1, waiting for transfers between devices, on_device(): full_rows = lax.all_gather(hidden, 'col', axis=0, tiled=True)  58.2 us
    all_gather x1, waiting for transfers between devices, on_device(): pair_all = lax.all_gather(pair_local, 'row', axis=1, tiled=True)  34.4 us
    all_to_all x1, blocking collectives, on_device(): merger_in = lax.all_to_all(merger_chunk, 'col', 0, 1, tiled=True)  14.1 us
    reduce_sum x1, other arithmetic, on_device(): merged_sum = jnp.sum(parts, axis=0)  12.2 us
  transfers between devices with their start and end apart: 5, of which 4 were waited for; matrix products, arithmetic and copies ran while one was open for 46% of the time, Pallas kernels for 0%

profile of v1, /device:TPU:0, one launch (start us, length us, event | category | flops | bytes accessed | tf_op | source)
XLA Modules:
  0.0 598.6 jit_solution(9178307829313079656)
XLA Ops:
  12.5 58.2 %all-gather.6.cloned.1.call-done = bf16[1408,2048]{1,0:T(8,128)(2,1)} async-done(((bf16[88,2048]{1,0:T(8,128)(2,1)}), bf16[1408,2048]{1,0:T(8,128)(2,1)}) %all-gather.6.cloned.1.call-update) | async-done | bytes 5767184 | tf_op jit(solution)/shard_map/all_gather | solution.py:31
  70.7 8.3 %copy.31 = bf16[1408,2048]{0,1:T(8,128)(2,1)} copy(bf16[1408,2048]{1,0:T(8,128)(2,1)} %all-gather.6.cloned.1.call-done) | data formatting | bytes 11534336 | tf_op jit(solution)/shard_map/all_gather | solution.py:31
  93.1 6.9 %scatter_fusion = bf16[2,88,2048]{1,0,2:T(2,128)(2,1)S(1)} fusion(bf16[2,88,2048]{1,0,2:T(2,128)(2,1)S(1)} %copy.33, s32[200]{0:T(256)S(1)} %bitcast.127, bf16[200,2,88]{2,1,0:T(2,128)(2,1)S(1)} %bitcast.120), kind=kCustom, calls=%fused_computation.2 | custom fusion | bytes 212000 | tf_op jit(solution)/shard_map/scatter | solution.py:50
  107.2 34.4 %all-gather.8.cloned.1.call-done = bf16[177,16384]{1,0:T(8,128)(2,1)} async-done(((bf16[177,2048]{1,0:T(8,128)(2,1)}), bf16[177,16384]{1,0:T(8,128)(2,1)}) %all-gather.8.cloned.1.call-update) | async-done | bytes 5799952 | tf_op jit(solution)/shard_map/all_gather | solution.py:56
  141.7 5.8 slice.29
  148.4 251.7 %while.18 = (s32[]{:T(128)}, f32[1,2048]{1,0:T(1,128)S(1)}, f32[1,2048]{1,0:T(1,128)S(1)}, f32[1,88,2048]{2,1,0:T(8,128)S(1)}, s32[2048]{0:T(1024)S(1)}, /*index...) while((s32[]{:T(128)}, f32[1,2048]{1,0:T(1,128)S(1)}, ...), condition=%wide.region_6.7_spmd.clone, body=%wide.region_3.0_spmd.clone.sunk | while | flops 768108544 | bytes 27504848 | solution.py:97
  148.5 5.6 fusion.45
  180.0 5.6 fusion.45
  211.6 5.6 fusion.45
  227.3 5.6 fusion.45
  243.0 5.6 fusion.45
  258.7 5.6 fusion.45
  274.4 5.6 fusion.45
  290.2 5.6 fusion.45
  305.9 5.6 fusion.45
  321.6 5.6 fusion.45
  353.0 5.6 fusion.45
  368.7 5.6 fusion.45
  384.4 5.6 fusion.45
  401.1 6.9 %all-to-all-start = ((bf16[88,16,128]{2,0,1:T(8,128)(2,1)}), bf16[88,16,128]{2,0,1:T(8,128)(2,1)S(1)}, u32[]{:S(2)}, u32[]{:S(2)}) async-start(bf16[88,16,128]{2,0,1:T(8,128)(2,1)} %copy.35), calls=%async_computation | async-start | bytes 720896 | tf_op jit(solution)/shard_map/all_to_all | solution.py:102
  408.1 7.6 %convert_element_type.52 = f32[1408,2048]{0,1:T(8,128)} convert(bf16[1408,2048]{0,1:T(8,128)(2,1)} %copy.31) | non-fusion elementwise | flops 2883584 | bytes 17301504 | tf_op jit(solution)/shard_map/convert_element_type | solution.py:33
  421.7 14.1 %all_to_all.35 = bf16[16,88,128]{2,1,0:T(8,128)(2,1)S(1)} all-to-all(bf16[16,88,128]{2,1,0:T(8,128)(2,1)S(1)} %bitcast.116), channel_id=1, replica_groups=mesh['row'=8,'col'=16] {'col'}, dimensions={0} | all-to-all | bytes 720896 | tf_op jit(solution)/shard_map/all_to_all | solution.py:115
  439.6 138.7 %all-gather.12.cloned.1.call-done = bf16[8192,1408]{1,0:T(8,128)(2,1)} async-done(((bf16[512,1408]{1,0:T(8,128)(2,1)}), bf16[8192,1408]{1,0:T(8,128)(2,1)}) %all-gather.12.cloned.1.call-update) | async-done | bytes 23068688 | tf_op jit(solution)/shard_map/all_gather | solution.py:120
  578.3 12.2 %reduce_sum.65 = bf16[512,1408]{1,0:T(8,128)(2,1)S(1)} reduce(bf16[16,512,1408]{2,1,0:T(8,128)(2,1)} %bitcast.109, bf16[]{:T(256)} %constant.104.clone.1), dimensions={0}, to_apply=%region_9.10 | reduce | flops 10813440 | bytes 24510466 | tf_op jit(solution)/shard_map/reduce_sum | solution.py:121
  (156 shorter events, 218.3 us)
Async XLA Ops:
  6.5 429.6 %copy-start = (bf16[4,88,1408]{2,1,0:T(8,128)(2,1)S(1)}, bf16[4,88,1408]{2,1,0:T(8,128)(2,1)}, u32[]{:S(2)}) copy-start(bf16[4,88,1408]{2,1,0:T(8,128)(2,1)} %param.22) | copy-start | bytes 2973700
  6.5 64.2 %all-gather.6.cloned.1.call-start = ((), (), s32[]{:S(2)}) async-start(), calls=%async_computation.2 | async-start | bytes 6127616 | tf_op jit(solution)/shard_map/all_gather | solution.py:31
  7.3 134.4 %all-gather.8.cloned.1.call-start = ((), (), s32[]{:S(2)}) async-start(), calls=%async_computation.3 | async-start | bytes 6782976 | tf_op jit(solution)/shard_map/all_gather | solution.py:56
  79.1 4.5 copy-start.1
  83.6 9.0 %copy-start.5 = (bf16[2,88,1408]{2,1,0:T(8,128)(2,1)S(1)}, bf16[2,88,1408]{2,1,0:T(8,128)(2,1)}, u32[]{:S(2)}) copy-start(bf16[2,88,1408]{2,1,0:T(8,128)(2,1)} %param.16) | copy-start | bytes 1486852
  87.5 15.0 %copy-start.3 = (bf16[88,1408]{1,0:T(8,128)(2,1)S(1)}, bf16[88,1408]{1,0:T(8,128)(2,1)}, u32[]{:S(2)}) copy-start(bf16[88,1408]{1,0:T(8,128)(2,1)} %param.15) | copy-start | bytes 743428
  101.8 313.8 %all-gather.10.cloned.1.call-start = ((), (), s32[]{:S(2)}) async-start(), calls=%async_computation.4 | async-start | bytes 4212736 | tf_op jit(solution)/shard_map/all_gather | solution.py:32
  102.5 45.9 %copy-start.2 = (s32[2048]{0:T(1024)S(1)}, s32[2048]{0:T(1024)}, u32[]{:S(2)}) copy-start(s32[2048]{0:T(1024)} %param.19) | copy-start | bytes 24580
  148.4 259.6 %copy-start.4 = (bf16[1408]{0:T(1024)(128)(2,1)S(1)}, bf16[1408]{0:T(1024)(128)(2,1)}, u32[]{:S(2)}) copy-start(bf16[1408]{0:T(1024)(128)(2,1)} %param.21) | copy-start | bytes 8452
  401.1 17.0 %all-to-all-start = ((bf16[88,16,128]{2,0,1:T(8,128)(2,1)}), bf16[88,16,128]{2,0,1:T(8,128)(2,1)S(1)}, u32[]{:S(2)}, u32[]{:S(2)}) async-start(bf16[88,16,128]{2,0,1:T(8,128)(2,1)} %copy.35), calls=%async_computation | async-start | bytes 720896 | tf_op jit(solution)/shard_map/all_to_all | solution.py:102
  408.0 170.4 %all-gather.12.cloned.1.call-start = ((), (), s32[]{:S(2)}) async-start(), calls=%async_computation.5 | async-start | bytes 24510464 | tf_op jit(solution)/shard_map/all_gather | solution.py:120
Sparse Core Ops, SparseCore 0:
  9.5 61.1 all-gather.5
  101.9 39.7 all-gather.7
  143.8 50.4 all-gather.9
  438.4 139.9 all-gather.11
